TPU v7x, 256 devices: a whole 4x4x8 slice. The times are simulated.
256 devices in a mesh: gx: 16 (over z, core), gy: 16 (over y, x).
Axes of the slice: x: 4, y: 4, z: 8, core: 2. Of those that a mesh axis runs over, the one named last changes fastest.
Arguments:
- demand: float32 [16, 1024, 16384], P(None, 'gx', 'gy'), may hold values from -200 to 200, as said below
- initial: float32 [1024, 256], replicated, may hold values from -6 to 6
Outputs:
- factor: float32 [1024, 256], replicated
- core: float32 [256, 16, 16384], P('gx', None, 'gy')
Inputs may be any that keep to these rules, and one draw needn't show every extreme that they name: `demand`: Real-valued fluctuations of order one to a few, not all of one scale along x.
All inputs are finite; a program needn't handle non-finite values.
Results may differ from a plain program's by a relative error of at most 0.0003.
Values sent between devices are 32-bit elements; how exact they have to be, the bound alone decides.
No kernel may reach another device: no remote copies, remote signals or barrier semaphores. Data moves between devices by JAX's collectives and lax.ppermute only.
A program may use at most 128 MiB of HBM per device.

v0:
```python
import jax
import jax.numpy as jnp
from jax import lax
from jax.sharding import PartitionSpec as P

NY = 1024
L = 16
S = 16
ITERS = 3


def orthonormal(block):
    weights = jnp.dot(
        block.T, block, precision=lax.Precision.HIGHEST, preferred_element_type=jnp.float32
    )
    lower_factor = jnp.linalg.cholesky(weights)
    return lax.linalg.triangular_solve(
        lower_factor, block, left_side=False, lower=True, transpose_a=True
    )


def on_device(demand, initial):
    regrouped = lax.all_to_all(demand, "gx", split_axis=0, concat_axis=1, tiled=True)
    local_gram = jnp.einsum(
        "lxc,lzc->xz",
        regrouped,
        regrouped,
        precision=lax.Precision.HIGHEST,
        preferred_element_type=jnp.float32,
    )
    local_gram = local_gram * (1.0 / (L * S * NY))
    basis = initial
    gram = lax.psum(local_gram, ("gx", "gy"))
    for iteration in range(ITERS):
        basis = orthonormal(
            jnp.dot(
                gram, basis, precision=lax.Precision.HIGHEST, preferred_element_type=jnp.float32
            )
        )
    core_part = jnp.einsum(
        "xr,lxc->rlc",
        basis,
        regrouped,
        precision=lax.Precision.HIGHEST,
        preferred_element_type=jnp.float32,
    )
    core = lax.all_to_all(core_part, "gx", split_axis=0, concat_axis=1, tiled=True)
    return (basis, core)


def solution(mesh):
    in_specs = (P(None, "gx", "gy"), P())
    out_specs = (P(), P("gx", None, "gy"))
    return jax.shard_map(
        on_device, mesh=mesh, in_specs=in_specs, out_specs=out_specs, check_vma=False
    )
```

profile of v0, /device:TPU:1, one launch (start us, length us, event | category | flops | bytes accessed | tf_op | source)
XLA Modules:
  0.0 658.2 jit_solution(15279910534653061629)
XLA Ops:
  7.2 106.0 %all_to_all.27 = f32[16,64,1024]{2,1,0:T(8,128)S(1)} all-to-all(f32[16,64,1024]{2,1,0:T(8,128)} %param.5), channel_id=1, replica_groups=mesh['gx'=16,'gy'=16] {'gx'}, dimensions={0} | all-to-all | bytes 8388608 | tf_op jit(solution)/shard_map/all_to_all | solution.py:23
  113.2 1.9 copy-done.1
  115.1 14.7 %convolution_multiply_fusion = f32[1024,1024]{1,0:T(8,128)} fusion(f32[1024,1024]{1,0:T(8,128)S(1)} %bitcast.118), kind=kOutput, calls=%fused_computation.6 | convolution fusion | flops 12885950464 | bytes 8388608 | tf_op jit(solution)/shard_map/lxc,lzc->xz/dot_general | solution.py:24
  129.9 265.4 %all-reduce.3.cloned.1.call-done = f32[1024,1024]{1,0:T(8,128)} async-done(((f32[1024,1024]{1,0:T(8,128)}), f32[1024,1024]{1,0:T(8,128)}) %all-reduce.3.cloned.1.call-update) | async-done | bytes 4194320 | tf_op jit(solution)/shard_map/psum | solution.py:33
  395.3 5.4 fusion.45
  400.7 1.8 fusion.46
  402.8 11.7 %cholesky.172 = f32[128,128]{1,0:T(8,128)S(1)} custom-call(f32[128,128]{1,0:T(8,128)S(1)} %cholesky.270), custom_call_target="Cholesky" | custom-call | tf_op jit(solution)/shard_map/jit(cholesky)/cholesky | solution.py:16
  414.5 9.8 %custom-call.15 = f32[1,128,128]{1,2,0:T(8,128)S(1)} custom-call(f32[1,128,128]{2,1,0:T(8,128)S(1)} %get-tuple-element.72), custom_call_target="InvertDiagBlocksLowerTriangular" | custom-call | tf_op jit(solution)/shard_map/jit(cholesky)/cholesky | solution.py:16
  424.4 0.2 constant_dynamic-update-slice_fusion.5
  424.6 0.3 convolution_subtract_fusion.5
  424.8 11.7 %cholesky.189 = f32[128,128]{1,0:T(8,128)S(1)} custom-call(f32[128,128]{1,0:T(8,128)S(1)} %convolution_subtract_fusion.5), custom_call_target="Cholesky" | custom-call | tf_op jit(solution)/shard_map/jit(cholesky)/cholesky | solution.py:16
  436.6 0.7 compare_reduce_fusion.4
  439.0 3.7 while.6
  439.0 0.6 fusion.77
  439.6 1.3 bitcast_dynamic-update-slice_fusion.6
  440.9 0.6 fusion.77
  441.4 1.3 bitcast_dynamic-update-slice_fusion.6
  442.7 19.7 %custom-call.16 = f32[2,128,128]{1,2,0:T(8,128)S(1)} custom-call(f32[2,128,128]{2,1,0:T(8,128)S(1)} %get-tuple-element.24), custom_call_target="InvertDiagBlocksLowerTriangular" | custom-call | tf_op jit(solution)/shard_map/triangular_solve/custom-call.0 | solution.py:17
  462.4 0.6 fusion.12
  463.1 1.0 convolution_subtract_fusion.2
  464.1 0.6 fusion.25
  464.7 5.3 fusion
  470.0 1.8 fusion.47
  472.1 11.7 %cholesky.206 = f32[128,128]{1,0:T(8,128)S(1)} custom-call(f32[128,128]{1,0:T(8,128)S(1)} %cholesky.273), custom_call_target="Cholesky" | custom-call | tf_op jit(solution)/shard_map/jit(cholesky)/cholesky | solution.py:16
  483.8 9.8 %custom-call.17 = f32[1,128,128]{1,2,0:T(8,128)S(1)} custom-call(f32[1,128,128]{2,1,0:T(8,128)S(1)} %get-tuple-element.68), custom_call_target="InvertDiagBlocksLowerTriangular" | custom-call | tf_op jit(solution)/shard_map/jit(cholesky)/cholesky | solution.py:16
  493.9 0.3 convolution_subtract_fusion.4
  494.1 11.7 %cholesky.223 = f32[128,128]{1,0:T(8,128)S(1)} custom-call(f32[128,128]{1,0:T(8,128)S(1)} %convolution_subtract_fusion.4), custom_call_target="Cholesky" | custom-call | tf_op jit(solution)/shard_map/jit(cholesky)/cholesky | solution.py:16
  505.9 0.6 compare_reduce_fusion.2
  506.5 0.6 compare_reduce_fusion.3
  508.6 3.8 while.7
  508.6 0.6 fusion.78
  509.2 1.3 bitcast_dynamic-update-slice_fusion.7
  510.5 0.6 fusion.78
  511.1 1.3 bitcast_dynamic-update-slice_fusion.7
  512.4 19.7 %custom-call.18 = f32[2,128,128]{1,2,0:T(8,128)S(1)} custom-call(f32[2,128,128]{2,1,0:T(8,128)S(1)} %get-tuple-element.25), custom_call_target="InvertDiagBlocksLowerTriangular" | custom-call | tf_op jit(solution)/shard_map/triangular_solve/custom-call.0 | solution.py:17
  532.1 0.6 fusion.10
  532.8 1.0 convolution_subtract_fusion.1
  533.8 0.6 fusion.21
  534.4 5.5 fusion.4
  540.0 1.8 fusion.48
  542.0 11.7 %cholesky.240 = f32[128,128]{1,0:T(8,128)S(1)} custom-call(f32[128,128]{1,0:T(8,128)S(1)} %cholesky.276), custom_call_target="Cholesky" | custom-call | tf_op jit(solution)/shard_map/jit(cholesky)/cholesky | solution.py:16
  553.8 9.8 %custom-call.19 = f32[1,128,128]{1,2,0:T(8,128)S(1)} custom-call(f32[1,128,128]{2,1,0:T(8,128)S(1)} %get-tuple-element.64), custom_call_target="InvertDiagBlocksLowerTriangular" | custom-call | tf_op jit(solution)/shard_map/jit(cholesky)/cholesky | solution.py:16
  563.6 0.2 constant_dynamic-update-slice_fusion
  563.8 0.3 convolution_subtract_fusion.3
  564.1 11.7 %cholesky.257 = f32[128,128]{1,0:T(8,128)S(1)} custom-call(f32[128,128]{1,0:T(8,128)S(1)} %convolution_subtract_fusion.3), custom_call_target="Cholesky" | custom-call | tf_op jit(solution)/shard_map/jit(cholesky)/cholesky | solution.py:16
  575.8 0.6 compare_reduce_fusion
  576.5 0.6 compare_reduce_fusion.1
  578.4 0.3 select_select_fusion
  578.7 3.9 while.8
  578.7 0.6 fusion.79
  579.3 1.4 bitcast_dynamic-update-slice_fusion.8
  580.7 0.6 fusion.79
  581.3 1.4 bitcast_dynamic-update-slice_fusion.8
  582.6 19.7 %custom-call.20 = f32[2,128,128]{1,2,0:T(8,128)S(1)} custom-call(f32[2,128,128]{2,1,0:T(8,128)S(1)} %get-tuple-element.26), custom_call_target="InvertDiagBlocksLowerTriangular" | custom-call | tf_op jit(solution)/shard_map/triangular_solve/custom-call.0 | solution.py:17
  602.3 0.6 fusion.8
  603.0 1.0 convolution_subtract_fusion
  604.0 0.6 fusion.17
  604.6 5.7 convolution_bitcast_fusion
  610.3 2.1 copy.12
  612.4 7.6 %all-to-all-start.1 = ((f32[256,1,1024]{2,1,0:T(1,128)}), f32[256,1,1024]{2,1,0:T(1,128)}, u32[]{:S(2)}, u32[]{:S(2)}) async-start(f32[256,1,1024]{2,1,0:T(1,128)} %copy.12), calls=%async_computation.1 | async-start | bytes 2097152 | tf_op jit(solution)/shard_map/all_to_all | solution.py:47
  620.0 1.0 pad_maximum_fusion
  621.1 2.5 copy.14
  623.6 24.5 %all-to-all-done.1 = f32[256,1,1024]{2,1,0:T(1,128)} async-done(((f32[256,1,1024]{2,1,0:T(1,128)}), f32[256,1,1024]{2,1,0:T(1,128)}, u32[]{:S(2)}, u32[]{:S(2)}) %all-to-all-start.1) | async-done | bytes 1048608 | tf_op jit(solution)/shard_map/all_to_all | solution.py:47
  648.1 2.8 copy.16
  (37 shorter events, 1.4 us)
Async XLA Ops:
  7.2 388.1 %copy-start = (f32[1024,256]{1,0:T(8,128)S(1)}, f32[1024,256]{1,0:T(8,128)}, u32[]{:S(2)}) copy-start(f32[1024,256]{1,0:T(8,128)} %param.6) | copy-start | bytes 3145732
  7.2 388.1 %all-reduce.3.cloned.1.call-start = ((), (), s32[]{:S(2)}) async-start(), calls=%async_computation.2 | async-start | bytes 8388608 | tf_op jit(solution)/shard_map/psum | solution.py:33
  113.2 1.9 copy-start.1
  612.4 35.7 %all-to-all-start.1 = ((f32[256,1,1024]{2,1,0:T(1,128)}), f32[256,1,1024]{2,1,0:T(1,128)}, u32[]{:S(2)}, u32[]{:S(2)}) async-start(f32[256,1,1024]{2,1,0:T(1,128)} %copy.12), calls=%async_computation.1 | async-start | bytes 2097152 | tf_op jit(solution)/shard_map/all_to_all | solution.py:47
Sparse Core Ops, SparseCore 0:
  130.0 265.2 all-reduce.2
where the time goes:
time: 665 us; the launch traced here: 658 us
  waiting for transfers between devices  290 us (44%)
  other arithmetic  164 us (25%)
  blocking collectives  106 us (16%)
  matrix products  50.4 us (8%)
  local copies, waits for them, and re-layouts  21.3 us (3%)
  between operations  18.9 us (3%)
  starting transfers between devices  7.65 us (1%)
    psum x1, waiting for transfers between devices, on_device(): gram = lax.psum(local_gram, ('gx', 'gy'))  265 us
    all_to_all x1, blocking collectives, on_device(): lax.all_to_all(demand, 'gx', split_axis=0, concat_axis=1, tiled=True)  106 us
    another operation x20, other arithmetic, orthonormal(): lower_factor = jnp.linalg.cholesky(weights)  103 us
    another operation x8, other arithmetic, orthonormal(): lax.linalg.triangular_solve(lower_factor, block, left_side=False, lower=T...  60.6 us
    all_to_all x1, waiting for transfers between devices, on_device(): lax.all_to_all(core_part, 'gx', split_axis=0, concat_axis=1, tiled=True)  24.5 us
    dot_general x3, matrix products, on_device(): jnp.dot(gram, basis, precision=lax.Precision.HIGHEST, preferred_element_t...  16.3 us
    dot_general x1, matrix products, on_device(): jnp.einsum('lxc,lzc->xz', regrouped, regrouped, precision=lax.Precision.H...  14.7 us
  transfers between devices with their start and end apart: 2, of which 2 were waited for; matrix products, arithmetic and copies ran while one was open for 1% of the time, Pallas kernels for 0%

commit v1 on v0

--- a/solution.py
+++ b/solution.py
@@ -30,7 +30,7 @@
     )
     local_gram = local_gram * (1.0 / (L * S * NY))
     basis = initial
-    gram = lax.psum(local_gram, ("gx", "gy"))
+    gram = lax.psum(lax.psum(local_gram, "gy"), "gx")
     for iteration in range(ITERS):
         basis = orthonormal(
             jnp.dot(

time: 665 us -> 633 us (0.952)
  waiting for transfers between devices: 290 us -> 258 us
    psum x1 -> x2, waiting for transfers between devices: 265 us -> 234 us  [on_device(): gram = lax.psum(lax.psum(local_gram, 'gy'), 'gx')]
  transfers between devices with their start and end apart: 2 -> 3, of which waited for: 2 -> 3; matrix products, arithmetic and copies ran while one was open for 1% -> 1% of each run, Pallas kernels for 0% -> 0%
where the time goes in v1:
time: 633 us; the launch traced here: 626 us
  waiting for transfers between devices  258 us (41%)
  other arithmetic  164 us (26%)
  blocking collectives  106 us (17%)
  matrix products  50.4 us (8%)
  local copies, waits for them, and re-layouts  21.3 us (3%)
  between operations  19 us (3%)
  starting transfers between devices  7.1 us (1%)
    psum x2, waiting for transfers between devices, on_device(): gram = lax.psum(lax.psum(local_gram, 'gy'), 'gx')  234 us
    all_to_all x1, blocking collectives, on_device(): lax.all_to_all(demand, 'gx', split_axis=0, concat_axis=1, tiled=True)  106 us
    another operation x20, other arithmetic, orthonormal(): lower_factor = jnp.linalg.cholesky(weights)  103 us
    another operation x8, other arithmetic, orthonormal(): lax.linalg.triangular_solve(lower_factor, block, left_side=False, lower=T...  60.6 us
    all_to_all x1, waiting for transfers between devices, on_device(): lax.all_to_all(core_part, 'gx', split_axis=0, concat_axis=1, tiled=True)  24.5 us
    dot_general x3, matrix products, on_device(): jnp.dot(gram, basis, precision=lax.Precision.HIGHEST, preferred_element_t...  16.3 us
    dot_general x1, matrix products, on_device(): jnp.einsum('lxc,lzc->xz', regrouped, regrouped, precision=lax.Precision.H...  14.8 us
  transfers between devices with their start and end apart: 3, of which 3 were waited for; matrix products, arithmetic and copies ran while one was open for 1% of the time, Pallas kernels for 0%

profile of v1, /device:TPU:1, one launch (start us, length us, event | category | flops | bytes accessed | tf_op | source)
XLA Modules:
  0.0 626.0 jit_solution(5665491487347921598)
XLA Ops:
  7.2 106.0 %all_to_all.27 = f32[16,64,1024]{2,1,0:T(8,128)S(1)} all-to-all(f32[16,64,1024]{2,1,0:T(8,128)} %param.5), channel_id=1, replica_groups=mesh['gx'=16,'gy'=16] {'gx'}, dimensions={0} | all-to-all | bytes 8388608 | tf_op jit(solution)/shard_map/all_to_all | solution.py:23
  113.2 1.9 copy-done.1
  115.1 14.8 %convolution_multiply_fusion = f32[1024,1024]{1,0:T(8,128)} fusion(f32[1024,1024]{1,0:T(8,128)S(1)} %bitcast.118), kind=kOutput, calls=%fused_computation.6 | convolution fusion | flops 12885950464 | bytes 8388608 | tf_op jit(solution)/shard_map/lxc,lzc->xz/dot_general | solution.py:24
  130.0 110.2 %all-reduce.4.cloned.1.call-done = f32[1024,1024]{1,0:T(8,128)} async-done(((f32[1024,1024]{1,0:T(8,128)}), f32[1024,1024]{1,0:T(8,128)}) %all-reduce.4.cloned.1.call-update) | async-done | bytes 4194320 | tf_op jit(solution)/shard_map/psum | solution.py:33
  240.2 123.5 %all-reduce.6.cloned.1.call-done = f32[1024,1024]{1,0:T(8,128)} async-done(((f32[1024,1024]{1,0:T(8,128)}), f32[1024,1024]{1,0:T(8,128)}) %all-reduce.6.cloned.1.call-update) | async-done | bytes 4194320 | tf_op jit(solution)/shard_map/psum | solution.py:33
  363.7 5.4 fusion.45
  369.1 1.8 fusion.46
  371.2 11.7 %cholesky.172 = f32[128,128]{1,0:T(8,128)S(1)} custom-call(f32[128,128]{1,0:T(8,128)S(1)} %cholesky.270), custom_call_target="Cholesky" | custom-call | tf_op jit(solution)/shard_map/jit(cholesky)/cholesky | solution.py:16
  382.9 9.8 %custom-call.15 = f32[1,128,128]{1,2,0:T(8,128)S(1)} custom-call(f32[1,128,128]{2,1,0:T(8,128)S(1)} %get-tuple-element.72), custom_call_target="InvertDiagBlocksLowerTriangular" | custom-call | tf_op jit(solution)/shard_map/jit(cholesky)/cholesky | solution.py:16
  393.0 0.3 convolution_subtract_fusion.5
  393.2 11.7 %cholesky.189 = f32[128,128]{1,0:T(8,128)S(1)} custom-call(f32[128,128]{1,0:T(8,128)S(1)} %convolution_subtract_fusion.5), custom_call_target="Cholesky" | custom-call | tf_op jit(solution)/shard_map/jit(cholesky)/cholesky | solution.py:16
  405.0 0.7 compare_reduce_fusion.4
  407.4 3.7 while.6
  407.4 0.6 fusion.77
  407.9 1.3 bitcast_dynamic-update-slice_fusion.6
  409.3 0.6 fusion.77
  409.8 1.3 bitcast_dynamic-update-slice_fusion.6
  411.1 19.7 %custom-call.16 = f32[2,128,128]{1,2,0:T(8,128)S(1)} custom-call(f32[2,128,128]{2,1,0:T(8,128)S(1)} %get-tuple-element.24), custom_call_target="InvertDiagBlocksLowerTriangular" | custom-call | tf_op jit(solution)/shard_map/triangular_solve/custom-call.0 | solution.py:17
  430.8 0.6 fusion.12
  431.4 1.0 convolution_subtract_fusion.2
  432.5 0.6 fusion.25
  433.1 5.3 fusion
  438.4 1.8 fusion.47
  440.5 11.7 %cholesky.206 = f32[128,128]{1,0:T(8,128)S(1)} custom-call(f32[128,128]{1,0:T(8,128)S(1)} %cholesky.273), custom_call_target="Cholesky" | custom-call | tf_op jit(solution)/shard_map/jit(cholesky)/cholesky | solution.py:16
  452.2 9.8 %custom-call.17 = f32[1,128,128]{1,2,0:T(8,128)S(1)} custom-call(f32[1,128,128]{2,1,0:T(8,128)S(1)} %get-tuple-element.68), custom_call_target="InvertDiagBlocksLowerTriangular" | custom-call | tf_op jit(solution)/shard_map/jit(cholesky)/cholesky | solution.py:16
  462.0 0.2 constant_dynamic-update-slice_fusion.3
  462.3 0.3 convolution_subtract_fusion.4
  462.5 11.7 %cholesky.223 = f32[128,128]{1,0:T(8,128)S(1)} custom-call(f32[128,128]{1,0:T(8,128)S(1)} %convolution_subtract_fusion.4), custom_call_target="Cholesky" | custom-call | tf_op jit(solution)/shard_map/jit(cholesky)/cholesky | solution.py:16
  474.3 0.6 compare_reduce_fusion.2
  474.9 0.6 compare_reduce_fusion.3
  477.0 3.8 while.7
  477.0 0.6 fusion.78
  477.6 1.3 bitcast_dynamic-update-slice_fusion.7
  478.9 0.6 fusion.78
  479.5 1.3 bitcast_dynamic-update-slice_fusion.7
  480.8 19.7 %custom-call.18 = f32[2,128,128]{1,2,0:T(8,128)S(1)} custom-call(f32[2,128,128]{2,1,0:T(8,128)S(1)} %get-tuple-element.25), custom_call_target="InvertDiagBlocksLowerTriangular" | custom-call | tf_op jit(solution)/shard_map/triangular_solve/custom-call.0 | solution.py:17
  500.5 0.6 fusion.10
  501.2 1.0 convolution_subtract_fusion.1
  502.2 0.6 fusion.21
  502.8 5.5 fusion.4
  508.3 1.8 fusion.48
  510.4 11.7 %cholesky.240 = f32[128,128]{1,0:T(8,128)S(1)} custom-call(f32[128,128]{1,0:T(8,128)S(1)} %cholesky.276), custom_call_target="Cholesky" | custom-call | tf_op jit(solution)/shard_map/jit(cholesky)/cholesky | solution.py:16
  522.2 9.8 %custom-call.19 = f32[1,128,128]{1,2,0:T(8,128)S(1)} custom-call(f32[1,128,128]{2,1,0:T(8,128)S(1)} %get-tuple-element.64), custom_call_target="InvertDiagBlocksLowerTriangular" | custom-call | tf_op jit(solution)/shard_map/jit(cholesky)/cholesky | solution.py:16
  532.2 0.3 convolution_subtract_fusion.3
  532.4 11.7 %cholesky.257 = f32[128,128]{1,0:T(8,128)S(1)} custom-call(f32[128,128]{1,0:T(8,128)S(1)} %convolution_subtract_fusion.3), custom_call_target="Cholesky" | custom-call | tf_op jit(solution)/shard_map/jit(cholesky)/cholesky | solution.py:16
  544.2 0.6 compare_reduce_fusion
  544.8 0.6 compare_reduce_fusion.1
  546.7 0.3 select_select_fusion
  547.1 3.9 while.8
  547.1 0.6 fusion.79
  547.7 1.4 bitcast_dynamic-update-slice_fusion.8
  549.1 0.6 fusion.79
  549.6 1.4 bitcast_dynamic-update-slice_fusion.8
  551.0 19.7 %custom-call.20 = f32[2,128,128]{1,2,0:T(8,128)S(1)} custom-call(f32[2,128,128]{2,1,0:T(8,128)S(1)} %get-tuple-element.26), custom_call_target="InvertDiagBlocksLowerTriangular" | custom-call | tf_op jit(solution)/shard_map/triangular_solve/custom-call.0 | solution.py:17
  570.7 0.6 fusion.8
  571.3 1.0 convolution_subtract_fusion
  572.3 0.6 fusion.17
  573.0 5.7 convolution_bitcast_fusion
  578.7 2.1 copy.12
  580.8 7.0 %all-to-all-start.1 = ((f32[256,1,1024]{2,1,0:T(1,128)}), f32[256,1,1024]{2,1,0:T(1,128)}, u32[]{:S(2)}, u32[]{:S(2)}) async-start(f32[256,1,1024]{2,1,0:T(1,128)} %copy.12), calls=%async_computation.1 | async-start | bytes 2097152 | tf_op jit(solution)/shard_map/all_to_all | solution.py:47
  587.8 1.1 pad_maximum_fusion
  588.9 2.5 copy.14
  591.4 24.5 %all-to-all-done.1 = f32[256,1,1024]{2,1,0:T(1,128)} async-done(((f32[256,1,1024]{2,1,0:T(1,128)}), f32[256,1,1024]{2,1,0:T(1,128)}, u32[]{:S(2)}, u32[]{:S(2)}) %all-to-all-start.1) | async-done | bytes 1048608 | tf_op jit(solution)/shard_map/all_to_all | solution.py:47
  615.9 2.8 copy.16
  (40 shorter events, 1.7 us)
Async XLA Ops:
  7.2 356.5 %copy-start = (f32[1024,256]{1,0:T(8,128)S(1)}, f32[1024,256]{1,0:T(8,128)}, u32[]{:S(2)}) copy-start(f32[1024,256]{1,0:T(8,128)} %param.6) | copy-start | bytes 3145732
  7.2 233.0 %all-reduce.4.cloned.1.call-start = ((), (), s32[]{:S(2)}) async-start(), calls=%async_computation.2 | async-start | bytes 8388608 | tf_op jit(solution)/shard_map/psum | solution.py:33
  113.2 1.9 copy-start.1
  129.9 233.8 %all-reduce.6.cloned.1.call-start = ((), (), s32[]{:S(2)}) async-start(), calls=%async_computation.3 | async-start | bytes 8388608 | tf_op jit(solution)/shard_map/psum | solution.py:33
  580.8 35.1 %all-to-all-start.1 = ((f32[256,1,1024]{2,1,0:T(1,128)}), f32[256,1,1024]{2,1,0:T(1,128)}, u32[]{:S(2)}, u32[]{:S(2)}) async-start(f32[256,1,1024]{2,1,0:T(1,128)} %copy.12), calls=%async_computation.1 | async-start | bytes 2097152 | tf_op jit(solution)/shard_map/all_to_all | solution.py:47
Sparse Core Ops, SparseCore 0:
  130.0 110.0 all-reduce.3
  242.5 121.1 all-reduce.5
